TPU v7x, 256 devices: a whole 4x4x8 slice. The times are simulated.
256 devices in a mesh: replica: 16 (over z_lo, x), fsdp: 16 (over y, z_hi, core).
Axes of the slice: x: 4, y: 4, z: 8 (z_hi: 2, z_lo: 4; z = z_hi * 4 + z_lo), core: 2. Of those that a mesh axis runs over, the one named last changes fastest.
Arguments:
- base: float32 [8192, 1024], P('fsdp'), may hold values from -6 to 6
- local: bfloat16 [16, 8192, 1024], P('replica', 'fsdp'), may hold values from -6 to 6
- momentum: float32 [8192, 1024], P('fsdp'), may hold values from -6 to 6
- tokens: bfloat16 [16, 2048, 8192], P('replica', 'fsdp'), may hold values from -6 to 6
- mask_embed: bfloat16 [8192], replicated, may hold values from -6 to 6
- mask_pos: int32 [16, 1, 768], P('replica'), may hold values from 0 to 2047, as said below
- cotangent: bfloat16 [16, 2048, 1024], P('replica', 'fsdp'), may hold values from -6 to 6
Outputs:
- new_momentum: bfloat16 [8192, 1024], P('fsdp')
- stepped: bfloat16 [16, 8192, 1024], P('replica', 'fsdp')
Inputs may be any that keep to these rules, and one draw needn't show every extreme that they name: `mask_pos`: each row holds 768 different positions of its sequence.
All inputs are finite; a program needn't handle non-finite values. Where the computation divides by a largest or mean magnitude, that divisor is 1e-20 or more.
Results may differ from a plain program's by a relative error of at most 0.008.
Values may be sent and summed in bfloat16 or wider, within the bound.
A program may use at most 128 MiB of HBM per device.

v0:
```python
import jax
import jax.numpy as jnp
from jax import lax
from jax.sharding import PartitionSpec as P

D = 8192
QBLOCK = 128
LENGTH = 2048


momentum_decay = 0.9
outer_rate = 0.7
inner_rate = 0.5


def body(base, local, momentum, tokens, mask_embed, mask_pos, cotangent):
    row_count, col_count = base.shape
    drift = base - local[0].astype(jnp.float32)
    blocks = drift.reshape(row_count, col_count // QBLOCK, QBLOCK)
    scales = (jnp.max(jnp.abs(blocks), axis=2, keepdims=True) + 1e-06).astype(jnp.bfloat16)
    code_vals = (blocks / scales.astype(jnp.float32)).astype(jnp.bfloat16)
    replicas = lax.axis_size("replica")
    dequant = (code_vals.astype(jnp.float32) * scales.astype(jnp.float32)).reshape(
        row_count, col_count
    )
    outer_grad = lax.psum(dequant, "replica") / replicas
    momentum_next = momentum_decay * momentum + outer_grad
    renewed = base - outer_rate * (outer_grad + momentum_decay * momentum_next)
    tok_rows = tokens.shape[1]
    offset = lax.axis_index("fsdp") * tok_rows
    places = offset + jnp.arange(tok_rows, dtype=jnp.int32)
    sequence = places // LENGTH
    position = places % LENGTH
    seq_ids = jnp.arange(mask_pos.shape[1], dtype=jnp.int32)
    matches = (mask_pos[0][None, :, :] == position[:, None, None]) & (
        sequence[:, None, None] == seq_ids[None, :, None]
    )
    masked = jnp.any(matches, axis=(1, 2))
    inputs = jnp.where(masked[:, None], mask_embed[None, :], tokens[0])
    upstream = cotangent[0]
    own_columns = lax.all_to_all(inputs, "fsdp", split_axis=1, concat_axis=0, tiled=True)
    all_upstream = lax.all_gather(upstream, "fsdp", axis=0, tiled=True)
    groups = lax.axis_size("fsdp")
    group_in = own_columns.reshape(groups, tok_rows, row_count)
    group_up = all_upstream.reshape(groups, tok_rows, col_count)

    def add_group(total, pair):
        term = lax.dot_general(
            pair[0], pair[1], (((0,), (0,)), ((), ())), preferred_element_type=jnp.float32
        )
        return (total + term.astype(jnp.bfloat16).astype(jnp.float32), None)

    grad_sum, _ = lax.scan(
        add_group, jnp.zeros((row_count, col_count), jnp.float32), (group_in, group_up)
    )
    gradient = grad_sum * D ** (-0.5)
    stepped = (renewed - inner_rate * gradient).astype(jnp.bfloat16)
    return (momentum_next.astype(jnp.bfloat16), stepped[None])


def solution(mesh):
    in_specs = (
        P("fsdp", None),
        P("replica", "fsdp", None),
        P("fsdp", None),
        P("replica", "fsdp", None),
        P(),
        P("replica", None, None),
        P("replica", "fsdp", None),
    )
    out_specs = (P("fsdp", None), P("replica", "fsdp", None))
    return jax.shard_map(body, mesh=mesh, in_specs=in_specs, out_specs=out_specs, check_vma=False)
```

profile of v0, /device:TPU:8, one launch (start us, length us, event | category | flops | bytes accessed | tf_op | source)
XLA Modules:
  0.0 255.8 jit_solution(18432817212518945594)
XLA Ops:
  8.8 3.2 %copy.18 = bf16[1,128,8192]{1,2,0:T(8,128)(2,1)S(1)} copy(bf16[1,128,8192]{2,1,0:T(8,128)(2,1)} %param.12) | data formatting | bytes 4194304 | tf_op args[3]
  12.3 2.2 broadcast_select_fusion
  14.5 11.8 %all-to-all-start = ((bf16[128,16,512]{0,2,1:T(8,128)(2,1)}), bf16[128,16,512]{0,2,1:T(8,128)(2,1)}, u32[]{:S(2)}, u32[]{:S(2)}) async-start(bf16[128,16,512]{0,2,1:T(8,128)(2,1)} %broadcast_select_fusion), calls=%async_computation | async-start | bytes 4194304 | tf_op jit(solution)/shard_map/all_to_all | solution.py:41
  26.8 1.8 copy.21
  28.6 2.2 reduce_max.9
  31.7 2.1 bitcast_multiply_fusion
  33.9 46.6 %all-to-all-done = bf16[128,16,512]{0,2,1:T(8,128)(2,1)} async-done(((bf16[128,16,512]{0,2,1:T(8,128)(2,1)}), bf16[128,16,512]{0,2,1:T(8,128)(2,1)}, u32[]{:S(2)}, u32[]{:S(2)}) %all-to-all-start) | async-done | bytes 2097184 | tf_op jit(solution)/shard_map/all_to_all | solution.py:41
  80.4 41.1 %all-gather.3.cloned.1.call-done = bf16[1,2048,1024]{2,1,0:T(8,128)(2,1)} async-done(((bf16[1,128,1024]{2,1,0:T(8,128)(2,1)}), bf16[1,2048,1024]{2,1,0:T(8,128)(2,1)}) %all-gather.3.cloned.1.call-update) | async-done | bytes 4194320 | tf_op jit(solution)/shard_map/all_gather | solution.py:42
  121.5 27.8 %while.11 = (s32[]{:T(128)}, f32[512,1024]{1,0:T(8,128)S(1)}, bf16[16,128,512]{1,2,0:T(8,128)(2,1)}, bf16[16,128,1024]{2,1,0:T(8,128)(2,1)}, s32[]{:T(128)}, /*index=5*/s32[]{:T(128)}) while((s32[]{:T(128)}, f32[512,1024]{1,0:T(8,128)S(1)}, bf16[16,128,512]{1,2,0:T(8,128)(2,1)}, bf16[16,128,1024]{2,1,0:T(8,128)(2,1)}, s32[]{:T(128)}, ...), condition=%wide.region_4.5_spmd.clone, body=%wide.region_3.4_spmd.clone.sunk | while | flops 136314880 | bytes 4588623 | solution.py:53
  123.3 1.7 select_add_fusion.2
  125.0 1.7 select_add_fusion.2
  126.7 1.7 select_add_fusion.2
  128.5 1.7 select_add_fusion.2
  130.2 1.7 select_add_fusion.2
  132.0 1.7 select_add_fusion.2
  133.7 1.7 select_add_fusion.2
  135.4 1.7 select_add_fusion.2
  137.2 1.7 select_add_fusion.2
  138.9 1.7 select_add_fusion.2
  142.4 1.7 select_add_fusion.2
  144.1 1.7 select_add_fusion.2
  147.6 1.7 select_add_fusion.2
  149.4 93.7 %all-reduce.2.cloned.1.call-done = f32[512,1024]{1,0:T(8,128)} async-done(((f32[512,1024]{1,0:T(8,128)}), f32[512,1024]{1,0:T(8,128)}) %all-reduce.2.cloned.1.call-update) | async-done | bytes 2097168 | tf_op jit(solution)/shard_map/psum | solution.py:26
  243.1 5.3 %fusion.7 = (bf16[1,512,1024]{2,1,0:T(8,128)(2,1)}, bf16[512,1024]{1,0:T(8,128)(2,1)}) fusion(f32[512,1024]{1,0:T(8,128)S(1)} %get-tuple-element.24, f32[512,1024]{1,0:T(8,128)} %param.9, f32[512,1024]{1,0:T(8,128)} %param.11, f32[512,1024]{1,0:T(8,128)} %all-reduce.2.cloned.1.call-done), kind=kLoop, calls=%fused_computation.16 | loop fusion | flops 5767168 | bytes 10485760 | tf_op jit(solution)/shard_map/broadcast_in_dim | solution.py:58
  (26 shorter events, 7.4 us)
Async XLA Ops:
  8.0 113.5 %all-gather.3.cloned.1.call-start = ((), (), s32[]{:S(2)}) async-start(), calls=%async_computation.2 | async-start | bytes 4456448 | tf_op jit(solution)/shard_map/all_gather | solution.py:42
  8.7 3.3 %copy-start.2 = (bf16[8192]{0:T(1024)(128)(2,1)S(1)}, bf16[8192]{0:T(1024)(128)(2,1)}, u32[]{:S(2)}) copy-start(bf16[8192]{0:T(1024)(128)(2,1)} %param.13) | copy-start | bytes 49156
  8.7 3.3 %copy-start.3 = (s32[1,1,768]{2,1,0:T(1,128)S(1)}, s32[1,1,768]{2,1,0:T(1,128)}, u32[]{:S(2)}) copy-start(s32[1,1,768]{2,1,0:T(1,128)} %param.14) | copy-start | bytes 9220
  14.5 11.9 %copy-start = (f32[512,1024]{1,0:T(8,128)S(1)}, f32[512,1024]{1,0:T(8,128)}, u32[]{:S(2)}) copy-start(f32[512,1024]{1,0:T(8,128)} %param.9) | copy-start | bytes 6291460
  14.5 11.9 %copy-start.1 = (bf16[1,512,1024]{2,1,0:T(8,128)(2,1)S(1)}, bf16[1,512,1024]{2,1,0:T(8,128)(2,1)}, u32[]{:S(2)}) copy-start(bf16[1,512,1024]{2,1,0:T(8,128)(2,1)} %param.10) | copy-start | bytes 3145732
  14.5 65.9 %all-to-all-start = ((bf16[128,16,512]{0,2,1:T(8,128)(2,1)}), bf16[128,16,512]{0,2,1:T(8,128)(2,1)}, u32[]{:S(2)}, u32[]{:S(2)}) async-start(bf16[128,16,512]{0,2,1:T(8,128)(2,1)} %broadcast_select_fusion), calls=%async_computation | async-start | bytes 4194304 | tf_op jit(solution)/shard_map/all_to_all | solution.py:41
  26.4 216.7 %all-reduce.2.cloned.1.call-start = ((), (), s32[]{:S(2)}) async-start(), calls=%async_computation.1 | async-start | bytes 4194304 | tf_op jit(solution)/shard_map/psum | solution.py:26
Sparse Core Ops, SparseCore 0:
  11.5 109.9 all-gather.2
Sparse Core Ops, SparseCore 1:
  33.9 209.1 all-reduce.1
where the time goes:
time: 256 us
  waiting for transfers between devices  182 us (71%)
  matrix products  27.5 us (11%)
  between operations  15.6 us (6%)
  other arithmetic  12.4 us (5%)
  starting transfers between devices  11.9 us (5%)
  local copies, waits for them, and re-layouts  5.93 us (2%)
    psum x1, waiting for transfers between devices, body(): outer_grad = lax.psum(dequant, 'replica') / replicas  93.7 us
    all_to_all x1, waiting for transfers between devices, body(): lax.all_to_all(inputs, 'fsdp', split_axis=1, concat_axis=0, tiled=True)  46.6 us
    all_gather x1, waiting for transfers between devices, body(): all_upstream = lax.all_gather(upstream, 'fsdp', axis=0, tiled=True)  41.1 us
    dot_general x16, matrix products, add_group(): lax.dot_general(pair[0], pair[1], (((0,), (0,)), ((), ())), preferred_ele...  27.5 us
    all_to_all x1, starting transfers between devices, body(): lax.all_to_all(inputs, 'fsdp', split_axis=1, concat_axis=0, tiled=True)  11.8 us
    broadcast_in_dim x1, other arithmetic, body(): return (momentum_next.astype(jnp.bfloat16), stepped[None])  5.25 us
  transfers between devices with their start and end apart: 3, of which 3 were waited for; matrix products, arithmetic and copies ran while one was open for 16% of the time, Pallas kernels for 0%

commit v1 on v0

v1 whole, which is shorter than its diff:
```python
import jax
import jax.numpy as jnp
from jax import lax
from jax.experimental import pallas as pl
from jax.experimental.pallas import tpu as pltpu
from jax.sharding import PartitionSpec as P

D = 8192
ROWS = 512
COLS = 1024
TOK = 128
QBLOCK = 128
NB = 4
CB = COLS // NB
NA = 4
CA = ROWS // NA
HALF = 1024

momentum_decay = 0.9
outer_rate = 0.7
inner_rate = 0.5

MESH = pl.DeviceIdType.MESH
BF = jnp.bfloat16
F32 = jnp.float32


def al(v, m):
    return pl.multiple_of(v, m)


def kernel(base_h, local_h, mom_h, tok_h, emb_ref, pos_ref, cot_h, nm_h, st_h,
           base_v, mom_v, lr, r2s, r2r, own, og, xa, xo, cb, mask_v, ev, ps, pr, q, nm_v, st_v,
           s_c, s_f, s_a, s_o, s_p, s_r1, s_r2, s_r3, s_r4,
           v_c, v_f, v_a, v_o, v_p, v_r1, v_r2, v_r3, v_r4, l_sem):
    r = lax.axis_index("replica")
    f = lax.axis_index("fsdp")
    zl, x = lax.div(r, 4), lax.rem(r, 4)
    y, h, c = lax.div(f, 4), lax.rem(lax.div(f, 2), 2), lax.rem(f, 2)
    slot = c * 4 + y

    def dev(zl_, x_, y_, h_, c_):
        return {"replica": zl_ * 4 + x_, "fsdp": y_ * 4 + h_ * 2 + c_}

    def half(k):
        t = lax.rem(slot + k, 8)
        return lax.rem(t, 4), lax.div(t, 4)

    def to_y(k):
        return dev(zl, x, lax.rem(y + k, 4), h, c)

    def to_x(k):
        return dev(zl, lax.rem(x + k, 4), y, h, c)

    def to_z(k):
        return dev(lax.rem(zl + k, 4), x, y, h, c)

    other_core = dev(zl, x, y, h, 1 - c)
    antipode = dev(zl, x, y, 1 - h, c)

    def send(src, dst, ss, rs, to):
        cp = pltpu.make_async_remote_copy(
            src_ref=src, dst_ref=dst, send_sem=ss, recv_sem=rs, device_id=to, device_id_type=MESH
        )
        cp.start()
        return cp

    def await_bytes(ref, sem):
        pltpu.make_async_copy(ref, ref, sem).wait()

    load_base = pltpu.make_async_copy(base_h, base_v, l_sem.at[0])
    load_mom = pltpu.make_async_copy(mom_h, mom_v, l_sem.at[1])
    load_base.start()
    load_mom.start()

    barrier = pltpu.get_barrier_semaphore()
    partners = [other_core, antipode]
    for k in (1, 2, 3):
        partners += [to_x(k), to_z(k)]
    for k in range(1, 8):
        yy, cc = half(k)
        partners.append(dev(zl, x, yy, h, cc))
    partners = partners[1:]
    for p in partners:
        pl.semaphore_signal(barrier, inc=1, device_id=p, device_id_type=MESH)
    pl.semaphore_wait(barrier, len(partners))

    sent = []

    def send_c(b):
        src = cot_h.at[0, :, pl.ds(b * CB, CB)]
        dst = cb.at[b, pl.ds(al(slot * TOK, TOK), TOK), :]
        for k in (2, 1, 3):
            sent.append(send(src, dst, s_c.at[b, k - 1], v_c.at[b], to_y(k)))
        pltpu.make_async_copy(src, dst, v_c.at[b]).start()

    def send_a(a):
        dst = xa.at[a, pl.ds(al(slot * TOK, TOK), TOK), :]
        for k in range(1, 8):
            yy, cc = half(k)
            col = al((yy * 4 + (1 - h) * 2 + cc) * ROWS + a * CA, CA)
            sent.append(send(tok_h.at[0, :, pl.ds(col, CA)], dst, s_a.at[a, k - 1], v_a.at[a], dev(zl, x, yy, h, cc)))
        col = al((y * 4 + (1 - h) * 2 + c) * ROWS + a * CA, CA)
        pltpu.make_async_copy(tok_h.at[0, :, pl.ds(col, CA)], dst, v_a.at[a]).start()

    def send_o():
        dst = xo.at[pl.ds(al(slot * TOK, TOK), TOK), :]
        for k in range(1, 8):
            yy, cc = half(k)
            col = al((yy * 4 + h * 2 + cc) * ROWS, ROWS)
            sent.append(send(tok_h.at[0, :, pl.ds(col, ROWS)], dst, s_o.at[k - 1], v_o, dev(zl, x, yy, h, cc)))
        col = al(f * ROWS, ROWS)
        pltpu.make_async_copy(tok_h.at[0, :, pl.ds(col, ROWS)], dst, v_o).start()

    def piece(k):
        return al(lax.rem(zl + 1 + k, 4) * 32, 32)

    def send_r1(k):
        dst = lr.at[x, pl.ds(piece(k), 32), :]
        for d in (2, 1, 3):
            row = al(lax.rem(x + d, 4) * 128 + piece(k), 32)
            sent.append(send(local_h.at[0, pl.ds(row, 32), :], dst, s_r1.at[k, d - 1], v_r1.at[k], to_x(d)))
        row = al(x * 128 + piece(k), 32)
        pltpu.make_async_copy(local_h.at[0, pl.ds(row, 32), :], dst, v_r1.at[k]).start()

    send_c(0)
    for i in range(4):
        send_r1(i)
        send_a(i)
    for b in (1, 2, 3):
        send_c(b)
    send_o()

    pos = pos_ref[0]

    def mask_slot(s, carry):
        first = (lax.rem(s, 4) * 4 + h * 2 + lax.div(s, 4)) * TOK
        place = first + lax.broadcasted_iota(jnp.int32, (TOK, 1), 0)
        hit = jnp.where(pos == place, 1.0, 0.0)
        any_hit = jnp.max(hit, axis=1, keepdims=True)
        mask_v[pl.ds(al(s * TOK, TOK), TOK), :] = jnp.broadcast_to(any_hit, (TOK, 128)).astype(BF)
        return carry

    lax.fori_loop(0, 8, mask_slot, 0)

    emb = emb_ref[...].astype(F32)
    blk = lax.broadcasted_iota(jnp.int32, (16, ROWS), 0)
    theirs = y * 4 + (1 - h) * 2 + c
    ev[0:1, :] = jnp.sum(jnp.where(blk == theirs, emb, 0.0), axis=0, keepdims=True)
    ev[1:2, :] = jnp.sum(jnp.where(blk == f, emb, 0.0), axis=0, keepdims=True)

    load_base.wait()

    def dequant(k):
        await_bytes(lr.at[:, pl.ds(piece(k), 32), :], v_r1.at[k])
        row = al(x * 128 + piece(k), 32)

        def block(i, carry):
            cols = pl.ds(al(i * QBLOCK, QBLOCK), QBLOCK)
            at = base_v[pl.ds(row, 32), cols]
            total = jnp.zeros((32, QBLOCK), F32)
            for s in range(4):
                drift = at - lr[s, pl.ds(piece(k), 32), cols].astype(F32)
                scale = (jnp.max(jnp.abs(drift), axis=1, keepdims=True) + 1e-6).astype(BF).astype(F32)
                code = (drift / scale).astype(BF).astype(F32)
                total = total + code * scale
            if k < 3:
                r2s[k, :, cols] = total.astype(BF)
            else:
                own[:, cols] = total
            return carry

        lax.fori_loop(0, COLS // QBLOCK, block, 0)
        if k < 3:
            sent.append(send(r2s.at[k], r2r.at[k], s_r2.at[k], v_r2.at[k], to_z(k + 1)))

    def forward_c(b):
        mine = pl.ds(al(c * 512, 512), 512)
        await_bytes(cb.at[b, mine, :], v_c.at[b])
        sent.append(send(cb.at[b, mine, :], cb.at[b, mine, :], s_f.at[b], v_f.at[b], other_core))

    def have_c(b):
        theirs_ = pl.ds(al((1 - c) * 512, 512), 512)
        await_bytes(cb.at[b, theirs_, :], v_f.at[b])

    def take_a(a):
        await_bytes(xa.at[a], v_a.at[a])
        fill = jnp.broadcast_to(ev[0:1, a * CA:(a + 1) * CA].astype(BF), (HALF, CA))
        xa[a] = jnp.where(mask_v[...] > 0, fill, xa[a])

    def term(lhs, b):
        return lax.dot_general(lhs, cb[b], (((0,), (0,)), ((), ())), preferred_element_type=F32)

    def partial(a, b):
        ps[b, pl.ds(al(a * CA, CA), CA), :] = term(xa[a], b).astype(BF)

    forward_c(0)
    for a in range(NA):
        dequant(a)
        if a == 0:
            have_c(0)
        take_a(a)
        partial(a, 0)
        part = pl.ds(a * CA, CA)
        sent.append(send(ps.at[0, part, :], pr.at[0, part, :], s_p.at[a], v_p.at[a], antipode))

    def column(b):
        def one(a, carry):
            partial(a, b)
            return carry

        have_c(b)
        lax.fori_loop(0, NA, one, 0)
        sent.append(send(ps.at[b], pr.at[b], s_p.at[3 + b], v_p.at[3 + b], antipode))

    forward_c(1)
    for k in range(3):
        await_bytes(r2r.at[k], v_r2.at[k])
    mine = pl.ds(al(x * 128 + zl * 32, 32), 32)
    total = own[...]
    for k in range(3):
        total = total + r2r[k].astype(F32)
    og[mine, :] = (total * (1.0 / 16.0)).astype(BF)
    for k in (1, 2, 3):
        sent.append(send(og.at[mine, :], og.at[mine, :], s_r3.at[k - 1], v_r3.at[k - 1], to_z(k)))
    column(1)
    forward_c(2)
    column(2)
    forward_c(3)
    for k in (1, 2, 3):
        row = al(x * 128 + lax.rem(zl + 4 - k, 4) * 32, 32)
        await_bytes(og.at[pl.ds(row, 32), :], v_r3.at[k - 1])
    rows_x = pl.ds(al(x * 128, 128), 128)
    for k in (1, 2, 3):
        sent.append(send(og.at[rows_x, :], og.at[rows_x, :], s_r4.at[k - 1], v_r4.at[k - 1], to_x(k)))
    column(3)

    await_bytes(xo, v_o)

    def fill_o(s, carry):
        rows = pl.ds(al(s * TOK, TOK), TOK)
        m = mask_v[rows, :] > 0
        for a in range(NA):
            cols = slice(a * CA, (a + 1) * CA)
            fill = jnp.broadcast_to(ev[1:2, cols].astype(BF), (TOK, CA))
            xo[rows, cols] = jnp.where(m, fill, xo[rows, cols])
        return carry

    lax.fori_loop(0, 8, fill_o, 0)

    def own_term(b, carry):
        for a in range(NA):
            q[b, a * CA:(a + 1) * CA, :] = term(xo[:, a * CA:(a + 1) * CA], b)
        return carry

    lax.fori_loop(0, NB, own_term, 0)

    for k in (1, 2, 3):
        row = al(lax.rem(x + 4 - k, 4) * 128, 128)
        await_bytes(og.at[pl.ds(row, 128), :], v_r4.at[k - 1])
    load_mom.wait()

    def outer(i, carry):
        rows = pl.ds(al(i * 32, 32), 32)
        grad = og[rows, :].astype(F32)
        after = momentum_decay * mom_v[rows, :] + grad
        nm_v[rows, :] = after.astype(BF)
        base_v[rows, :] = base_v[rows, :] - outer_rate * (grad + momentum_decay * after)
        return carry

    lax.fori_loop(0, 16, outer, 0)
    store_nm = pltpu.make_async_copy(nm_v, nm_h, l_sem.at[2])
    store_nm.start()

    for cp in sent:
        cp.wait_send()

    stores = []

    def finish(b, lo, n):
        rows = slice(lo, lo + n)
        cols = slice(b * CB, (b + 1) * CB)
        gradient = (q[b, rows, :] + pr[b, rows, :].astype(F32)) * D ** (-0.5)
        st_v[rows, cols] = (base_v[rows, cols] - inner_rate * gradient).astype(BF)

    for a in range(NA):
        await_bytes(pr.at[0, pl.ds(a * CA, CA), :], v_p.at[a])
        finish(0, a * CA, CA)
    for b in (1, 2, 3):
        await_bytes(pr.at[b], v_p.at[3 + b])
        finish(b, 0, ROWS)
    store_st = pltpu.make_async_copy(st_v, st_h.at[0], l_sem.at[3])
    store_st.start()
    store_nm.wait()
    store_st.wait()


def body(base, local, momentum, tokens, mask_embed, mask_pos, cotangent):
    hbm = pl.BlockSpec(memory_space=pl.ANY)
    vmem = pl.BlockSpec(memory_space=pltpu.VMEM)
    dma = pltpu.SemaphoreType.DMA
    new_momentum, stepped = pl.pallas_call(
        kernel,
        name="step",
        out_shape=(
            jax.ShapeDtypeStruct((ROWS, COLS), BF),
            jax.ShapeDtypeStruct((1, ROWS, COLS), BF),
        ),
        in_specs=[hbm, hbm, hbm, hbm, vmem, vmem, hbm],
        out_specs=(hbm, hbm),
        scratch_shapes=[
            pltpu.VMEM((ROWS, COLS), F32),
            pltpu.VMEM((ROWS, COLS), F32),
            pltpu.VMEM((4, 128, COLS), BF),
            pltpu.VMEM((3, 32, COLS), BF),
            pltpu.VMEM((3, 32, COLS), BF),
            pltpu.VMEM((32, COLS), F32),
            pltpu.VMEM((ROWS, COLS), BF),
            pltpu.VMEM((NA, HALF, CA), BF),
            pltpu.VMEM((HALF, ROWS), BF),
            pltpu.VMEM((NB, HALF, CB), BF),
            pltpu.VMEM((HALF, 128), BF),
            pltpu.VMEM((8, ROWS), F32),
            pltpu.VMEM((NB, ROWS, CB), BF),
            pltpu.VMEM((NB, ROWS, CB), BF),
            pltpu.VMEM((NB, ROWS, CB), F32),
            pltpu.VMEM((ROWS, COLS), BF),
            pltpu.VMEM((ROWS, COLS), BF),
            dma((NB, 3)),
            dma((NB,)),
            dma((NA, 7)),
            dma((7,)),
            dma((7,)),
            dma((4, 3)),
            dma((3,)),
            dma((3,)),
            dma((3,)),
            dma((NB,)),
            dma((NB,)),
            dma((NA,)),
            dma(()),
            dma((7,)),
            dma((4,)),
            dma((3,)),
            dma((3,)),
            dma((3,)),
            dma((4,)),
        ],
        compiler_params=pltpu.CompilerParams(
            collective_id=0, has_side_effects=True, vmem_limit_bytes=48 * 2**20
        ),
    )(base, local, momentum, tokens, mask_embed.reshape(16, ROWS), mask_pos, cotangent)
    return new_momentum, stepped


def solution(mesh):
    in_specs = (
        P("fsdp", None),
        P("replica", "fsdp", None),
        P("fsdp", None),
        P("replica", "fsdp", None),
        P(),
        P("replica", None, None),
        P("replica", "fsdp", None),
    )
    out_specs = (P("fsdp", None), P("replica", "fsdp", None))
    return jax.shard_map(body, mesh=mesh, in_specs=in_specs, out_specs=out_specs, check_vma=False)
```

time: 256 us -> 98.9 us (0.39)
  the two profiles are of different devices: /device:TPU:8 before, /device:TPU:51 now
where the time goes in v1:
time: 98.9 us; the launch traced here: 98.6 us
  Pallas kernels  90.9 us (92%)
  local copies, waits for them, and re-layouts  7.13 us (7%)
    pallas_call x1, Pallas kernels, body(): pl.pallas_call(kernel, name='step', out_shape=(jax.ShapeDtypeStruct((ROWS...  90.9 us
    unnamed x10, local copies, waits for them, and re-layouts  6.39 us

profile of v1, /device:TPU:51, one launch (start us, length us, event | category | flops | bytes accessed | tf_op | source)
XLA Modules:
  0.0 98.6 jit_solution(8952882566149866122)
XLA Ops:
  0.6 0.7 reshape.7.emb_ref
  1.4 0.0 copy-start
  1.4 1.6 %copy-done = f32[512,1024]{1,0:T(8,128)S(1)} copy-done((f32[512,1024]{1,0:T(8,128)S(1)}, f32[512,1024]{1,0:T(8,128)}, u32[]{:S(2)}) %copy-start) | copy-done | bytes 2097176
  3.0 0.0 copy-start.1
  3.0 1.2 %copy-done.1 = bf16[1,512,1024]{2,1,0:T(8,128)(2,1)S(1)} copy-done((bf16[1,512,1024]{2,1,0:T(8,128)(2,1)S(1)}, bf16[1,512,1024]{2,1,0:T(8,128)(2,1)}, u32[]{:S(2)}) %copy-start.1) | copy-done | bytes 1048600
  4.2 0.0 copy-start.2
  4.2 0.9 copy-done.2
  5.1 0.0 copy-start.3
  5.1 0.7 copy-done.3
  5.8 90.9 %step.1 = (bf16[512,1024]{1,0:T(8,128)(2,1)S(1)}, bf16[1,512,1024]{2,1,0:T(8,128)(2,1)S(1)}) custom-call(f32[512,1024]{1,0:T(8,128)S(1)} %copy-done, bf16[1,512,1024]{2,1,0:T(8,128)(2,1)S(1)} %copy-done.1, f32[512,1024]{1,0:T(8,128)} %mom_h.1, bf16[1,128,8192]{2,1,0:T(8,128)(2,1)} %tok_h.1, bf16[16,512]{1,0:T(8,128)(2,1)S(1)} %reshape.7.emb_ref, ...), custom_call_target="tpu_custom_call" | custom-call | tf_op jit(solution)/shard_map/step/pallas_call | solution.py:302
  96.7 1.0 copy.11
  97.7 1.0 copy.12
Async XLA Ops:
  1.4 1.6 %copy-start = (f32[512,1024]{1,0:T(8,128)S(1)}, f32[512,1024]{1,0:T(8,128)}, u32[]{:S(2)}) copy-start(f32[512,1024]{1,0:T(8,128)} %base_h.1) | copy-start | bytes 6291460
  3.0 1.2 %copy-start.1 = (bf16[1,512,1024]{2,1,0:T(8,128)(2,1)S(1)}, bf16[1,512,1024]{2,1,0:T(8,128)(2,1)}, u32[]{:S(2)}) copy-start(bf16[1,512,1024]{2,1,0:T(8,128)(2,1)} %local_h.1) | copy-start | bytes 3145732
  4.2 0.9 copy-start.2
  5.1 0.7 copy-start.3

commit v2 on v1

--- a/solution.py
+++ b/solution.py
@@ -29,8 +29,8 @@
     return pl.multiple_of(v, m)
 
 
-def kernel(base_h, local_h, mom_h, tok_h, emb_ref, pos_ref, cot_h, nm_h, st_h,
-           base_v, mom_v, lr, r2s, r2r, own, og, xa, xo, cb, mask_v, ev, ps, pr, q, nm_v, st_v,
+def kernel(base_h, local_h, mom_h, tok_h, emb_ref, pos_h, cot_h, nm_v, st_v,
+           base_v, mom_v, lr, r2s, r2r, own, og, xa, xo, cb, mask_v, ev, ps, pr, q, pos_v,
            s_c, s_f, s_a, s_o, s_p, s_r1, s_r2, s_r3, s_r4,
            v_c, v_f, v_a, v_o, v_p, v_r1, v_r2, v_r3, v_r4, l_sem):
     r = lax.axis_index("replica")
@@ -70,6 +70,8 @@
 
     load_base = pltpu.make_async_copy(base_h, base_v, l_sem.at[0])
     load_mom = pltpu.make_async_copy(mom_h, mom_v, l_sem.at[1])
+    load_pos = pltpu.make_async_copy(pos_h, pos_v, l_sem.at[2])
+    load_pos.start()
     load_base.start()
     load_mom.start()
 
@@ -131,7 +133,8 @@
         send_c(b)
     send_o()
 
-    pos = pos_ref[0]
+    load_pos.wait()
+    pos = pos_v[0]
 
     def mask_slot(s, carry):
         first = (lax.rem(s, 4) * 4 + h * 2 + lax.div(s, 4)) * TOK
@@ -202,18 +205,20 @@
         take_a(a)
         partial(a, 0)
         part = pl.ds(a * CA, CA)
-        sent.append(send(ps.at[0, part, :], pr.at[0, part, :], s_p.at[a], v_p.at[a], antipode))
+        send(ps.at[0, part, :], pr.at[0, part, :], s_p.at[0, a], v_p.at[0, a], antipode)
 
     def column(b):
         def one(a, carry):
             partial(a, b)
+            rows = pl.ds(al(a * CA, CA), CA)
+            send(ps.at[b, rows, :], pr.at[b, rows, :], s_p.at[b, a], v_p.at[b, a], antipode)
             return carry
 
         have_c(b)
         lax.fori_loop(0, NA, one, 0)
-        sent.append(send(ps.at[b], pr.at[b], s_p.at[3 + b], v_p.at[3 + b], antipode))
 
     forward_c(1)
+    column(1)
     for k in range(3):
         await_bytes(r2r.at[k], v_r2.at[k])
     mine = pl.ds(al(x * 128 + zl * 32, 32), 32)
@@ -223,9 +228,7 @@
     og[mine, :] = (total * (1.0 / 16.0)).astype(BF)
     for k in (1, 2, 3):
         sent.append(send(og.at[mine, :], og.at[mine, :], s_r3.at[k - 1], v_r3.at[k - 1], to_z(k)))
-    column(1)
     forward_c(2)
-    column(2)
     forward_c(3)
     for k in (1, 2, 3):
         row = al(x * 128 + lax.rem(zl + 4 - k, 4) * 32, 32)
@@ -233,8 +236,9 @@
     rows_x = pl.ds(al(x * 128, 128), 128)
     for k in (1, 2, 3):
         sent.append(send(og.at[rows_x, :], og.at[rows_x, :], s_r4.at[k - 1], v_r4.at[k - 1], to_x(k)))
+
+    column(2)
     column(3)
-
     await_bytes(xo, v_o)
 
     def fill_o(s, carry):
@@ -269,34 +273,26 @@
         return carry
 
     lax.fori_loop(0, 16, outer, 0)
-    store_nm = pltpu.make_async_copy(nm_v, nm_h, l_sem.at[2])
-    store_nm.start()
 
     for cp in sent:
         cp.wait_send()
-
-    stores = []
 
     def finish(b, lo, n):
         rows = slice(lo, lo + n)
         cols = slice(b * CB, (b + 1) * CB)
         gradient = (q[b, rows, :] + pr[b, rows, :].astype(F32)) * D ** (-0.5)
-        st_v[rows, cols] = (base_v[rows, cols] - inner_rate * gradient).astype(BF)
-
-    for a in range(NA):
-        await_bytes(pr.at[0, pl.ds(a * CA, CA), :], v_p.at[a])
-        finish(0, a * CA, CA)
-    for b in (1, 2, 3):
-        await_bytes(pr.at[b], v_p.at[3 + b])
-        finish(b, 0, ROWS)
-    store_st = pltpu.make_async_copy(st_v, st_h.at[0], l_sem.at[3])
-    store_st.start()
-    store_nm.wait()
-    store_st.wait()
+        st_v[0, rows, cols] = (base_v[rows, cols] - inner_rate * gradient).astype(BF)
+
+    for b in range(NB):
+        for a in range(NA):
+            part = pl.ds(a * CA, CA)
+            await_bytes(pr.at[b, part, :], v_p.at[b, a])
+            finish(b, a * CA, CA)
+            await_bytes(ps.at[b, part, :], s_p.at[b, a])
 
 
 def body(base, local, momentum, tokens, mask_embed, mask_pos, cotangent):
-    hbm = pl.BlockSpec(memory_space=pl.ANY)
+    hbm = pl.BlockSpec(memory_space=pltpu.HBM)
     vmem = pl.BlockSpec(memory_space=pltpu.VMEM)
     dma = pltpu.SemaphoreType.DMA
     new_momentum, stepped = pl.pallas_call(
@@ -306,8 +302,8 @@
             jax.ShapeDtypeStruct((ROWS, COLS), BF),
             jax.ShapeDtypeStruct((1, ROWS, COLS), BF),
         ),
-        in_specs=[hbm, hbm, hbm, hbm, vmem, vmem, hbm],
-        out_specs=(hbm, hbm),
+        in_specs=[hbm, hbm, hbm, hbm, vmem, hbm, hbm],
+        out_specs=(vmem, vmem),
         scratch_shapes=[
             pltpu.VMEM((ROWS, COLS), F32),
             pltpu.VMEM((ROWS, COLS), F32),
@@ -324,13 +320,12 @@
             pltpu.VMEM((NB, ROWS, CB), BF),
             pltpu.VMEM((NB, ROWS, CB), BF),
             pltpu.VMEM((NB, ROWS, CB), F32),
-            pltpu.VMEM((ROWS, COLS), BF),
-            pltpu.VMEM((ROWS, COLS), BF),
+            pltpu.VMEM((1, 1, 768), jnp.int32),
             dma((NB, 3)),
             dma((NB,)),
             dma((NA, 7)),
             dma((7,)),
-            dma((7,)),
+            dma((NB, NA)),
             dma((4, 3)),
             dma((3,)),
             dma((3,)),
@@ -339,15 +334,15 @@
             dma((NB,)),
             dma((NA,)),
             dma(()),
-            dma((7,)),
+            dma((NB, NA)),
             dma((4,)),
             dma((3,)),
             dma((3,)),
             dma((3,)),
-            dma((4,)),
+            dma((3,)),
         ],
         compiler_params=pltpu.CompilerParams(
-            collective_id=0, has_side_effects=True, vmem_limit_bytes=48 * 2**20
+            collective_id=0, has_side_effects=True, vmem_limit_bytes=60 * 2**20
         ),
     )(base, local, momentum, tokens, mask_embed.reshape(16, ROWS), mask_pos, cotangent)
     return new_momentum, stepped

time: 98.9 us -> 85.5 us (0.86)
  the two profiles are of different devices: /device:TPU:51 before, /device:TPU:99 now
where the time goes in v2:
time: 85.5 us; the launch traced here: 85.2 us
  Pallas kernels  79.9 us (93%)
  local copies, waits for them, and re-layouts  4.67 us (5%)
    pallas_call x1, Pallas kernels, body(): pl.pallas_call(kernel, name='step', out_shape=(jax.ShapeDtypeStruct((ROWS...  79.9 us
    unnamed x4, local copies, waits for them, and re-layouts  3.32 us

profile of v2, /device:TPU:99, one launch (start us, length us, event | category | flops | bytes accessed | tf_op | source)
XLA Modules:
  0.0 85.2 jit_solution(14506501476032806910)
XLA Ops:
  0.6 1.3 %reshape.7.emb_ref = bf16[16,512]{1,0:T(8,128)(2,1)} reshape(bf16[8192]{0:T(1024)(128)(2,1)} %param.11) | data formatting | bytes 32768 | tf_op jit(solution)/shard_map/reshape | solution.py:347
  2.0 79.9 %step.1 = (bf16[512,1024]{1,0:T(8,128)(2,1)}, bf16[1,512,1024]{2,1,0:T(8,128)(2,1)}) custom-call(f32[512,1024]{1,0:T(8,128)} %base_h.1, bf16[1,512,1024]{2,1,0:T(8,128)(2,1)} %local_h.1, f32[512,1024]{1,0:T(8,128)} %mom_h.1, bf16[1,128,8192]{2,1,0:T(8,128)(2,1)} %tok_h.1, bf16[16,512]{1,0:T(8,128)(2,1)} %reshape.7.emb_ref, s32[1,1,768]{2,1,0:T(1,128)} %pos_h.1, ...), custom_call_target="tpu_custom_call" | custom-call | tf_op jit(solution)/shard_map/step/pallas_call | solution.py:298
  81.9 0.0 copy-start
  81.9 2.4 %copy.11 = bf16[512,1024]{1,0:T(8,128)(2,1)} copy(bf16[512,1024]{1,0:T(8,128)(2,1)} %get-tuple-element.4) | data formatting | bytes 2097152
  84.2 0.0 copy-done
  84.2 1.0 %copy.12 = bf16[1,512,1024]{2,1,0:T(8,128)(2,1)} copy(bf16[1,512,1024]{2,1,0:T(8,128)(2,1)S(1)} %copy-done) | data formatting | bytes 2097152
Async XLA Ops:
  81.9 2.4 %copy-start = (bf16[1,512,1024]{2,1,0:T(8,128)(2,1)S(1)}, bf16[1,512,1024]{2,1,0:T(8,128)(2,1)}, u32[]{:S(2)}) copy-start(bf16[1,512,1024]{2,1,0:T(8,128)(2,1)} %get-tuple-element.5) | copy-start | bytes 3145732

commit v3 on v2

--- a/solution.py
+++ b/solution.py
@@ -29,8 +29,8 @@
     return pl.multiple_of(v, m)
 
 
-def kernel(base_h, local_h, mom_h, tok_h, emb_ref, pos_h, cot_h, nm_v, st_v,
-           base_v, mom_v, lr, r2s, r2r, own, og, xa, xo, cb, mask_v, ev, ps, pr, q, pos_v,
+def kernel(base_h, local_h, mom_h, tok_h, emb_h, pos_h, cot_h, nm_v, st_v,
+           base_v, mom_v, lr, r2s, r2r, own, og, xa, xo, cb, mask_v, ev, ps, pr, q, pos_v, emb_v,
            s_c, s_f, s_a, s_o, s_p, s_r1, s_r2, s_r3, s_r4,
            v_c, v_f, v_a, v_o, v_p, v_r1, v_r2, v_r3, v_r4, l_sem):
     r = lax.axis_index("replica")
@@ -72,6 +72,8 @@
     load_mom = pltpu.make_async_copy(mom_h, mom_v, l_sem.at[1])
     load_pos = pltpu.make_async_copy(pos_h, pos_v, l_sem.at[2])
     load_pos.start()
+    load_emb = pltpu.make_async_copy(emb_h, emb_v, l_sem.at[3])
+    load_emb.start()
     load_base.start()
     load_mom.start()
 
@@ -146,11 +148,14 @@
 
     lax.fori_loop(0, 8, mask_slot, 0)
 
-    emb = emb_ref[...].astype(F32)
-    blk = lax.broadcasted_iota(jnp.int32, (16, ROWS), 0)
+    load_emb.wait()
+    emb = emb_v[...].astype(F32)
+    line = lax.broadcasted_iota(jnp.int32, (64, 128), 0)
     theirs = y * 4 + (1 - h) * 2 + c
-    ev[0:1, :] = jnp.sum(jnp.where(blk == theirs, emb, 0.0), axis=0, keepdims=True)
-    ev[1:2, :] = jnp.sum(jnp.where(blk == f, emb, 0.0), axis=0, keepdims=True)
+    for a in range(NA):
+        cols = slice(a * CA, (a + 1) * CA)
+        ev[0:1, cols] = jnp.sum(jnp.where(line == theirs * NA + a, emb, 0.0), axis=0, keepdims=True)
+        ev[1:2, cols] = jnp.sum(jnp.where(line == f * NA + a, emb, 0.0), axis=0, keepdims=True)
 
     load_base.wait()
 
@@ -293,17 +298,16 @@
 
 def body(base, local, momentum, tokens, mask_embed, mask_pos, cotangent):
     hbm = pl.BlockSpec(memory_space=pltpu.HBM)
-    vmem = pl.BlockSpec(memory_space=pltpu.VMEM)
     dma = pltpu.SemaphoreType.DMA
     new_momentum, stepped = pl.pallas_call(
         kernel,
         name="step",
         out_shape=(
-            jax.ShapeDtypeStruct((ROWS, COLS), BF),
-            jax.ShapeDtypeStruct((1, ROWS, COLS), BF),
+            pltpu.VMEM((ROWS, COLS), BF),
+            pltpu.VMEM((1, ROWS, COLS), BF),
         ),
-        in_specs=[hbm, hbm, hbm, hbm, vmem, hbm, hbm],
-        out_specs=(vmem, vmem),
+        in_specs=[hbm] * 7,
+        out_specs=(pl.BlockSpec(memory_space=pltpu.VMEM),) * 2,
         scratch_shapes=[
             pltpu.VMEM((ROWS, COLS), F32),
             pltpu.VMEM((ROWS, COLS), F32),
@@ -321,6 +325,7 @@
             pltpu.VMEM((NB, ROWS, CB), BF),
             pltpu.VMEM((NB, ROWS, CB), F32),
             pltpu.VMEM((1, 1, 768), jnp.int32),
+            pltpu.VMEM((64, 128), BF),
             dma((NB, 3)),
             dma((NB,)),
             dma((NA, 7)),
@@ -339,12 +344,12 @@
             dma((3,)),
             dma((3,)),
             dma((3,)),
-            dma((3,)),
+            dma((4,)),
         ],
         compiler_params=pltpu.CompilerParams(
             collective_id=0, has_side_effects=True, vmem_limit_bytes=60 * 2**20
         ),
-    )(base, local, momentum, tokens, mask_embed.reshape(16, ROWS), mask_pos, cotangent)
+    )(base, local, momentum, tokens, mask_embed.reshape(64, 128), mask_pos, cotangent)
     return new_momentum, stepped
 
 

time: 85.5 us -> 80.8 us (0.945)
  local copies, waits for them, and re-layouts: 4.67 us -> 1.94 us
  Pallas kernels: 79.9 us -> 78.2 us
    pallas_call x1, Pallas kernels: 79.9 us -> 78.2 us  [body(): pl.pallas_call(kernel, name='step', out_shape=(pltpu.VMEM((ROWS, COLS), B...]
    unnamed x4 -> x2, local copies, waits for them, and re-layouts: 3.32 us -> 1.94 us
    reshape x1 -> x0, local copies, waits for them, and re-layouts: 1.34 us -> none  [body(): mask_embed.reshape(16, ROWS)]
where the time goes in v3:
time: 80.8 us
  Pallas kernels  78.2 us (97%)
  local copies, waits for them, and re-layouts  1.94 us (2%)
    pallas_call x1, Pallas kernels, body(): pl.pallas_call(kernel, name='step', out_shape=(pltpu.VMEM((ROWS, COLS), B...  78.2 us
    unnamed x2, local copies, waits for them, and re-layouts  1.94 us

profile of v3, /device:TPU:99, one launch (start us, length us, event | category | flops | bytes accessed | tf_op | source)
XLA Modules:
  0.0 80.8 jit_solution(17649809451095641196)
XLA Ops:
  0.6 78.2 %step.1 = (bf16[512,1024]{1,0:T(8,128)(2,1)S(1)}, bf16[1,512,1024]{2,1,0:T(8,128)(2,1)S(1)}) custom-call(f32[512,1024]{1,0:T(8,128)} %base_h.1, bf16[1,512,1024]{2,1,0:T(8,128)(2,1)} %local_h.1, f32[512,1024]{1,0:T(8,128)} %mom_h.1, bf16[1,128,8192]{2,1,0:T(8,128)(2,1)} %tok_h.1, bf16[64,128]{1,0:T(8,128)(2,1)} %bitcast.1, s32[1,1,768]{2,1,0:T(1,128)} %pos_h.1, ...), custom_call_target="tpu_custom_call" | custom-call | tf_op jit(solution)/shard_map/step/pallas_call | solution.py:302
  78.8 1.0 %copy.11 = bf16[512,1024]{1,0:T(8,128)(2,1)} copy(bf16[512,1024]{1,0:T(8,128)(2,1)S(1)} %get-tuple-element.2) | data formatting | bytes 2097152
  79.8 1.0 %copy.12 = bf16[1,512,1024]{2,1,0:T(8,128)(2,1)} copy(bf16[1,512,1024]{2,1,0:T(8,128)(2,1)S(1)} %get-tuple-element.3) | data formatting | bytes 2097152

commit v4 on v3

--- a/solution.py
+++ b/solution.py
@@ -116,8 +116,13 @@
         col = al(f * ROWS, ROWS)
         pltpu.make_async_copy(tok_h.at[0, :, pl.ds(col, ROWS)], dst, v_o).start()
 
+    zb, zp = lax.rem(zl, 2), lax.div(zl, 2)
+    near = dev(zl + 1 - 2 * zb, x, y, h, c)
+    far = dev(zl + 2 - 4 * zp, x, y, h, c)
+    owners = (3 - zb - 2 * zp, 1 - zb + 2 * zp, zb + 2 - 2 * zp, zl)
+
     def piece(k):
-        return al(lax.rem(zl + 1 + k, 4) * 32, 32)
+        return al(owners[k] * 32, 32)
 
     def send_r1(k):
         dst = lr.at[x, pl.ds(piece(k), 32), :]
@@ -162,6 +167,8 @@
     def dequant(k):
         await_bytes(lr.at[:, pl.ds(piece(k), 32), :], v_r1.at[k])
         row = al(x * 128 + piece(k), 32)
+        if k == 2:
+            await_bytes(r2r.at[0], v_r2.at[0])
 
         def block(i, carry):
             cols = pl.ds(al(i * QBLOCK, QBLOCK), QBLOCK)
@@ -172,6 +179,8 @@
                 scale = (jnp.max(jnp.abs(drift), axis=1, keepdims=True) + 1e-6).astype(BF).astype(F32)
                 code = (drift / scale).astype(BF).astype(F32)
                 total = total + code * scale
+            if k == 2:
+                total = total + r2r[0, :, cols].astype(F32)
             if k < 3:
                 r2s[k, :, cols] = total.astype(BF)
             else:
@@ -180,7 +189,7 @@
 
         lax.fori_loop(0, COLS // QBLOCK, block, 0)
         if k < 3:
-            sent.append(send(r2s.at[k], r2r.at[k], s_r2.at[k], v_r2.at[k], to_z(k + 1)))
+            sent.append(send(r2s.at[k], r2r.at[k], s_r2.at[k], v_r2.at[k], near if k < 2 else far))
 
     def forward_c(b):
         mine = pl.ds(al(c * 512, 512), 512)
@@ -212,23 +221,24 @@
         part = pl.ds(a * CA, CA)
         send(ps.at[0, part, :], pr.at[0, part, :], s_p.at[0, a], v_p.at[0, a], antipode)
 
-    def column(b):
+    def column(b, first=0, last=NA):
         def one(a, carry):
             partial(a, b)
             rows = pl.ds(al(a * CA, CA), CA)
             send(ps.at[b, rows, :], pr.at[b, rows, :], s_p.at[b, a], v_p.at[b, a], antipode)
             return carry
 
-        have_c(b)
-        lax.fori_loop(0, NA, one, 0)
+        if first == 0:
+            have_c(b)
+        lax.fori_loop(first, last, one, 0)
 
     forward_c(1)
-    column(1)
-    for k in range(3):
+    column(1, 0, 2)
+    for k in (1, 2):
         await_bytes(r2r.at[k], v_r2.at[k])
     mine = pl.ds(al(x * 128 + zl * 32, 32), 32)
     total = own[...]
-    for k in range(3):
+    for k in (1, 2):
         total = total + r2r[k].astype(F32)
     og[mine, :] = (total * (1.0 / 16.0)).astype(BF)
     for k in (1, 2, 3):
@@ -242,6 +252,7 @@
     for k in (1, 2, 3):
         sent.append(send(og.at[rows_x, :], og.at[rows_x, :], s_r4.at[k - 1], v_r4.at[k - 1], to_x(k)))
 
+    column(1, 2, NA)
     column(2)
     column(3)
     await_bytes(xo, v_o)

time: 80.8 us -> 80 us (0.990)
  the two profiles are of different devices: /device:TPU:99 before, /device:TPU:64 now
where the time goes in v4:
time: 80 us; the launch traced here: 79.9 us
  Pallas kernels  77.3 us (97%)
  local copies, waits for them, and re-layouts  1.94 us (2%)
    pallas_call x1, Pallas kernels, body(): pl.pallas_call(kernel, name='step', out_shape=(pltpu.VMEM((ROWS, COLS), B...  77.3 us
    unnamed x2, local copies, waits for them, and re-layouts  1.94 us

profile of v4, /device:TPU:64, one launch (start us, length us, event | category | flops | bytes accessed | tf_op | source)
XLA Modules:
  0.0 79.9 jit_solution(12063472435015901007)
XLA Ops:
  0.6 77.3 %step.1 = (bf16[512,1024]{1,0:T(8,128)(2,1)S(1)}, bf16[1,512,1024]{2,1,0:T(8,128)(2,1)S(1)}) custom-call(f32[512,1024]{1,0:T(8,128)} %base_h.1, bf16[1,512,1024]{2,1,0:T(8,128)(2,1)} %local_h.1, f32[512,1024]{1,0:T(8,128)} %mom_h.1, bf16[1,128,8192]{2,1,0:T(8,128)(2,1)} %tok_h.1, bf16[64,128]{1,0:T(8,128)(2,1)} %bitcast.1, s32[1,1,768]{2,1,0:T(1,128)} %pos_h.1, ...), custom_call_target="tpu_custom_call" | custom-call | tf_op jit(solution)/shard_map/step/pallas_call | solution.py:313
  78.0 1.0 %copy.11 = bf16[512,1024]{1,0:T(8,128)(2,1)} copy(bf16[512,1024]{1,0:T(8,128)(2,1)S(1)} %get-tuple-element.2) | data formatting | bytes 2097152
  79.0 1.0 %copy.12 = bf16[1,512,1024]{2,1,0:T(8,128)(2,1)} copy(bf16[1,512,1024]{2,1,0:T(8,128)(2,1)S(1)} %get-tuple-element.3) | data formatting | bytes 2097152

commit v5 on v4

--- a/solution.py
+++ b/solution.py
@@ -233,7 +233,7 @@
         lax.fori_loop(first, last, one, 0)
 
     forward_c(1)
-    column(1, 0, 2)
+    column(1, 0, 1)
     for k in (1, 2):
         await_bytes(r2r.at[k], v_r2.at[k])
     mine = pl.ds(al(x * 128 + zl * 32, 32), 32)
@@ -252,7 +252,7 @@
     for k in (1, 2, 3):
         sent.append(send(og.at[rows_x, :], og.at[rows_x, :], s_r4.at[k - 1], v_r4.at[k - 1], to_x(k)))
 
-    column(1, 2, NA)
+    column(1, 1, NA)
     column(2)
     column(3)
     await_bytes(xo, v_o)

time: 80 us -> 79.7 us (level)
  no operation moved by 1% of the time
where the time goes in v5:
time: 79.7 us; the launch traced here: 79.6 us
  Pallas kernels  77 us (97%)
  local copies, waits for them, and re-layouts  1.94 us (2%)
    pallas_call x1, Pallas kernels, body(): pl.pallas_call(kernel, name='step', out_shape=(pltpu.VMEM((ROWS, COLS), B...  77 us
    unnamed x2, local copies, waits for them, and re-layouts  1.94 us

profile of v5, /device:TPU:64, one launch (start us, length us, event | category | flops | bytes accessed | tf_op | source)
XLA Modules:
  0.0 79.6 jit_solution(3966485666187417897)
XLA Ops:
  0.6 77.0 %step.1 = (bf16[512,1024]{1,0:T(8,128)(2,1)S(1)}, bf16[1,512,1024]{2,1,0:T(8,128)(2,1)S(1)}) custom-call(f32[512,1024]{1,0:T(8,128)} %base_h.1, bf16[1,512,1024]{2,1,0:T(8,128)(2,1)} %local_h.1, f32[512,1024]{1,0:T(8,128)} %mom_h.1, bf16[1,128,8192]{2,1,0:T(8,128)(2,1)} %tok_h.1, bf16[64,128]{1,0:T(8,128)(2,1)} %bitcast.1, s32[1,1,768]{2,1,0:T(1,128)} %pos_h.1, ...), custom_call_target="tpu_custom_call" | custom-call | tf_op jit(solution)/shard_map/step/pallas_call | solution.py:313
  77.7 1.0 %copy.11 = bf16[512,1024]{1,0:T(8,128)(2,1)} copy(bf16[512,1024]{1,0:T(8,128)(2,1)S(1)} %get-tuple-element.2) | data formatting | bytes 2097152
  78.7 1.0 %copy.12 = bf16[1,512,1024]{2,1,0:T(8,128)(2,1)} copy(bf16[1,512,1024]{2,1,0:T(8,128)(2,1)S(1)} %get-tuple-element.3) | data formatting | bytes 2097152

commit v6 on v5

--- a/solution.py
+++ b/solution.py
@@ -134,8 +134,8 @@
 
     send_c(0)
     for i in range(4):
+        send_a(i)
         send_r1(i)
-        send_a(i)
     for b in (1, 2, 3):
         send_c(b)
     send_o()

time: 79.7 us -> 79.7 us (level)
  no operation moved by 1% of the time
where the time goes in v6:
time: 79.7 us; the launch traced here: 79.6 us
  Pallas kernels  77 us (97%)
  local copies, waits for them, and re-layouts  1.94 us (2%)
    pallas_call x1, Pallas kernels, body(): pl.pallas_call(kernel, name='step', out_shape=(pltpu.VMEM((ROWS, COLS), B...  77 us
    unnamed x2, local copies, waits for them, and re-layouts  1.94 us

profile of v6, /device:TPU:64, one launch (start us, length us, event | category | flops | bytes accessed | tf_op | source)
XLA Modules:
  0.0 79.6 jit_solution(755152973759189083)
XLA Ops:
  0.6 77.0 %step.1 = (bf16[512,1024]{1,0:T(8,128)(2,1)S(1)}, bf16[1,512,1024]{2,1,0:T(8,128)(2,1)S(1)}) custom-call(f32[512,1024]{1,0:T(8,128)} %base_h.1, bf16[1,512,1024]{2,1,0:T(8,128)(2,1)} %local_h.1, f32[512,1024]{1,0:T(8,128)} %mom_h.1, bf16[1,128,8192]{2,1,0:T(8,128)(2,1)} %tok_h.1, bf16[64,128]{1,0:T(8,128)(2,1)} %bitcast.1, s32[1,1,768]{2,1,0:T(1,128)} %pos_h.1, ...), custom_call_target="tpu_custom_call" | custom-call | tf_op jit(solution)/shard_map/step/pallas_call | solution.py:313
  77.7 1.0 %copy.11 = bf16[512,1024]{1,0:T(8,128)(2,1)} copy(bf16[512,1024]{1,0:T(8,128)(2,1)S(1)} %get-tuple-element.2) | data formatting | bytes 2097152
  78.7 1.0 %copy.12 = bf16[1,512,1024]{2,1,0:T(8,128)(2,1)} copy(bf16[1,512,1024]{2,1,0:T(8,128)(2,1)S(1)} %get-tuple-element.3) | data formatting | bytes 2097152
